TPU v7x, 32 devices: a whole 2x2x4 slice. The times are simulated.
32 devices in a mesh: groups: 2 (over y), ctx: 4 (over x, core), chan: 4 (over z).
Axes of the slice: x: 2, y: 2, z: 4, core: 2. Of those that a mesh axis runs over, the one named last changes fastest.
Arguments:
- stream: bfloat16 [1536, 4096], P(('groups', 'ctx'), 'chan'), parts along dimension 0, may hold values from -30 to 30
- in_weights: bfloat16 [2, 4096, 3, 2048], P(None, 'ctx', None, 'chan'), may hold values from -0.09375 to 0.09375
- out_weights: bfloat16 [2, 4096, 2048], P(None, 'ctx', 'chan'), may hold values from -0.125 to 0.125
- short_taps: bfloat16 [7, 2048], P(None, 'chan'), may hold values from -2.390625 to 2.390625
- medium_taps: bfloat16 [128, 128], P(None, 'chan'), may hold values from -0.5390625 to 0.5390625
- plan: int32 [4], replicated, may hold values from 0 to 1
Outputs:
- result: bfloat16 [1536, 4096], P(('groups', 'ctx'), 'chan'), parts along dimension 0
There are 2 independent parts, one for each index of `groups`. A program takes and returns all parts, laid end to end along the dimension named above; an argument that names none is the same for every part. Nothing has to cross between parts.
All inputs are finite; a program needn't handle non-finite values.
Results may differ from a plain program's by a relative error of at most 0.03.
Values may be sent and summed in bfloat16 or wider, within the bound.
A program may use at most 128 MiB of HBM per device.

v0:
```python
from functools import partial

import jax
import jax.numpy as jnp
from jax import lax
from jax.experimental import pallas as pl
from jax.experimental.pallas import tpu as pltpu
from jax.sharding import PartitionSpec as P

STEPS = 4


def passed_along(value, axis, steps):
    count = lax.axis_size(axis)
    leading, last = (max(0, -steps), min(count, count - steps))
    return lax.ppermute(value, axis, [(source, source + steps) for source in range(leading, last)])


def section_taps(section, short_taps, medium_taps):
    reach = medium_taps.shape[0]
    channels = short_taps.shape[1]
    padding = jnp.zeros((reach - short_taps.shape[0], channels), short_taps.dtype)
    short_full = jnp.concatenate([short_taps, padding], 0)
    group_size = channels // medium_taps.shape[1]
    medium_full = jnp.broadcast_to(
        medium_taps[:, :, None], (reach, medium_taps.shape[1], group_size)
    ).reshape(reach, channels)
    return jnp.where(section == 0, short_full, medium_full)


def causal_filter(extended, filter_taps):
    filtered = lax.conv_general_dilated(
        extended[None],
        filter_taps[::-1][:, None, :],
        (1,),
        "VALID",
        dimension_numbers=("NWC", "WIO", "NWC"),
        feature_group_count=filter_taps.shape[1],
        preferred_element_type=jnp.float32,
    )
    return filtered[0]


def filter_gate(projected, section, short_taps, medium_taps):
    query_bf = projected[:, 0].astype(jnp.bfloat16)
    mixed_bf = (projected[:, 1] * projected[:, 2]).astype(jnp.bfloat16)
    reach = medium_taps.shape[0]
    earlier = passed_along(mixed_bf[-reach:], "ctx", 1)
    extended = jnp.concatenate([earlier[1:], mixed_bf], 0)
    filtered = causal_filter(extended, section_taps(section, short_taps, medium_taps))
    return (query_bf.astype(jnp.float32) * filtered).astype(jnp.bfloat16)


def expand_rows(hidden):
    return lax.all_gather(hidden, "chan", axis=1, tiled=True)


def combine(hidden, partial_sum):
    update = lax.psum_scatter(
        partial_sum.astype(jnp.bfloat16), "chan", scatter_dimension=1, tiled=True
    ).astype(jnp.float32)
    return (hidden.astype(jnp.float32) + update).astype(jnp.bfloat16)


def advance(hidden, section, project, emit, short_taps, medium_taps):
    full_rows = expand_rows(hidden)
    widened = full_rows.astype(jnp.float32)
    row_scale = lax.rsqrt(jnp.mean(widened * widened, axis=1, keepdims=True) + 1e-05)
    projected, kept_in = project(full_rows, section)
    projected = projected.reshape(full_rows.shape[0], 3, -1) * row_scale[:, :, None]
    gated_bf = filter_gate(projected, section, short_taps, medium_taps)
    partial_sum, kept_out = emit(gated_bf, section)
    return (combine(hidden, partial_sum), kept_in, kept_out)


def stored_project(weights_in, full_rows, section):
    chosen = lax.dynamic_index_in_dim(weights_in, section, 0, keepdims=False)
    projected = jnp.dot(
        full_rows, chosen.reshape(chosen.shape[0], -1), preferred_element_type=jnp.float32
    )
    return (projected, weights_in)


def stored_emit(weights_out, gated_bf, section):
    chosen = lax.dynamic_index_in_dim(weights_out, section, 0, keepdims=False)
    product = lax.dot_general(
        gated_bf, chosen, (((1,), (1,)), ((), ())), preferred_element_type=jnp.float32
    )
    return (product, weights_out)


def shards(stream, in_weights, out_weights, short_taps, medium_taps, plan):
    hidden = stream
    weights_in, weights_out = (
        lax.all_gather(in_weights, "ctx", axis=1, tiled=True),
        lax.all_gather(out_weights, "ctx", axis=1, tiled=True),
    )
    first_step = 0
    for step_index in range(first_step, STEPS):
        hidden, weights_in, weights_out = advance(
            hidden,
            plan[step_index],
            partial(stored_project, weights_in),
            partial(stored_emit, weights_out),
            short_taps,
            medium_taps,
        )
    return hidden


CHUNKS = 6
SKEW = 2
ENTRY = 9
PAD = 128
LANES = 128
BF = jnp.bfloat16
F32 = jnp.float32


def stationary_kernel(
    sizes, plan, stream, w_in, w_out, taps, out,
    h, p_send, p_recv, x_send, x_recv, own, ss_own, ss_recv, mixed, query, gat, acc, r_send, r_recv,
    init_s, init_r, ss_s, ss_r, p_s, p_r, x_s, x_r, g_s, g_r, r_s, r_r, b_s, b_r, o_s, o_r, local_sem,
):
    tokens, rows, block, width, half = sizes
    ctx, chan = lax.axis_index("ctx"), lax.axis_index("chan")
    n_ctx, n_chan = 4, 4
    side, core = ctx // 2, ctx % 2
    partner = {"ctx": side * 2 + (1 - core)}
    across = {"ctx": (1 - side) * 2 + core}
    diagonal = {"ctx": (1 - side) * 2 + (1 - core)}
    relations = (partner, across, diagonal)
    last = n_chan - 1
    place = (chan, last - chan)
    onward = ({"chan": jnp.minimum(chan + 1, last)}, {"chan": jnp.maximum(chan - 1, 0)})
    back = (onward[1], onward[0])

    def remote(source, target, send, recv, device):
        return pltpu.make_async_remote_copy(
            src_ref=source, dst_ref=target, send_sem=send, recv_sem=recv,
            device_id=device, device_id_type=pl.DeviceIdType.MESH,
        )

    barrier = pltpu.get_barrier_semaphore()
    for di in range(n_ctx):
        for dk in range(n_chan):
            if di or dk:
                pl.semaphore_signal(
                    barrier, inc=1,
                    device_id={"ctx": (ctx + di) % n_ctx, "chan": (chan + dk) % n_chan},
                    device_id_type=pl.DeviceIdType.MESH,
                )
    pl.semaphore_wait(barrier, n_ctx * n_chan - 1)

    block_rows = tokens // n_ctx
    mine = pl.ds(pl.multiple_of(ctx * block_rows, block_rows), block_rows)

    def init_copy(kappa):
        return remote(stream, h.at[mine, :], init_s.at[kappa], init_r.at[ctx], {"ctx": chan, "chan": kappa})

    def init_wait(source):
        there = pl.ds(source * block_rows, block_rows)
        return remote(stream, h.at[there, :], init_s.at[0], init_r.at[source], {"ctx": chan, "chan": 0})

    corner = ctx == chan
    for kappa in range(n_chan):
        @pl.when(jnp.logical_not(corner & (chan == kappa)))
        def _():
            init_copy(kappa).start()

    @pl.when(corner)
    def _():
        keep = pltpu.make_async_copy(stream, h.at[mine, :], local_sem)
        keep.start()
        keep.wait()

    mixed[pl.ds(0, PAD), :] = jnp.zeros((PAD, LANES), F32)
    for source in range(n_ctx):
        @pl.when(jnp.logical_not(corner & (ctx == source)))
        def _():
            init_wait(source).wait_recv()
    for kappa in range(n_chan):
        @pl.when(jnp.logical_not(corner & (chan == kappa)))
        def _():
            init_copy(kappa).wait_send()

    def span(t):
        return pl.ds(pl.multiple_of(t * rows, rows), rows)

    def ss_copy(rel, t):
        return remote(ss_own.at[t], ss_recv.at[rel, t], ss_s.at[rel, t], ss_r.at[rel, t], relations[rel])

    def p_copy(slot, t):
        return remote(p_send.at[slot, t], p_recv.at[slot, t], p_s.at[slot, t], p_r.at[slot, t], partner)

    def x_copy(t):
        return remote(x_send.at[t], x_recv.at[t], x_s.at[t], x_r.at[t], across)

    def lanes(index):
        return pl.ds(pl.multiple_of(index * LANES, LANES), LANES)

    def g_copy(kind, t, sending=True):
        owner = (1 - side) * 2 + core if kind == 2 else ctx
        if not sending:
            owner = (across["ctx"], partner["ctx"], diagonal["ctx"])[kind]
        ref = gat.at[span(t), lanes(owner)]
        return remote(ref, ref, g_s.at[kind, t], g_r.at[kind, t], across if kind == 0 else partner)

    def r_copy(d, t):
        return remote(r_send.at[d, t], r_recv.at[d, t], r_s.at[d, t], r_r.at[d, t], onward[d])

    def b_copy(d, t):
        ref = h.at[span(t), pl.ds(d * half, half)]
        return remote(ref, ref, b_s.at[d, t], b_r.at[d, t], back[d])

    def arrive(t):
        for d in range(2):
            @pl.when(place[d] == 0)
            def _():
                b_copy(d, t).wait_recv()

    def each(count, body):
        def wrapped(t, carry):
            body(t)
            return carry
        lax.fori_loop(0, count, wrapped, 0)

    def project(section, t, index):
        columns = lanes(index)
        weights = jnp.concatenate([w_in[section, j, :, columns] for j in range(3)], 1)
        return jnp.dot(h[span(t), :], weights, preferred_element_type=F32)

    def enter(section, t):
        p_send[0, t] = project(section, t, diagonal["ctx"]).astype(BF)
        p_copy(0, t).start()
        p_send[1, t] = project(section, t, partner["ctx"]).astype(BF)
        p_copy(1, t).start()
        wide = h[span(t), :].astype(F32)
        squares = (wide * wide).astype(BF)
        ss_own[t] = lax.dot_general(
            jnp.ones((8, squares.shape[1]), BF), squares, (((1,), (1,)), ((), ())), preferred_element_type=F32
        )
        for rel in range(3):
            ss_copy(rel, t).start()

    def cross(section, t):
        passing = project(section, t, across["ctx"])
        p_copy(0, t).wait_recv()
        x_send[t] = (passing + p_recv[0, t].astype(F32)).astype(BF)
        x_copy(t).start()
        own[t] = project(section, t, ctx)

    def entering(s, u):
        section = plan[s]

        @pl.when((u >= 0) & (u < CHUNKS))
        def _():
            @pl.when(s > 0)
            def _():
                arrive(u)

            enter(section, u)

        @pl.when((u > 0) & (u <= CHUNKS))
        def _():
            cross(section, u - 1)

    def step(s, carry):
        section = plan[s]

        def mix(t):
            for rel in range(3):
                ss_copy(rel, t).wait_recv()
            p_copy(1, t).wait_recv()
            x_copy(t).wait_recv()
            total = ss_own[t] + ss_recv[0, t] + ss_recv[1, t] + ss_recv[2, t]
            scale = lax.rsqrt(total * (1.0 / width) + 1e-05)
            scale = jnp.transpose(scale)[:, :1]
            parts = (own[t] + p_recv[1, t].astype(F32) + x_recv[t].astype(F32)) * scale
            query = parts[:, :LANES].astype(BF).astype(F32)
            product = parts[:, LANES:2 * LANES] * parts[:, 2 * LANES:]
            mixed[pl.ds(pl.multiple_of(PAD + t * rows, rows), rows), :] = product.astype(BF).astype(F32)

            def tap_block(jj, total):
                start = pl.multiple_of(PAD + t * rows - 8 * jj - 8, 8)
                window = mixed[pl.ds(start, rows + 8), :]
                weights = taps[section, jj]
                for c in range(8):
                    total = total + weights[c:c + 1, :] * window[8 - c:8 - c + rows, :]
                return total

            filtered = lax.fori_loop(0, taps.shape[1], tap_block, jnp.zeros((rows, LANES), F32))
            gat[span(t), lanes(ctx)] = (query * filtered).astype(BF)
            g_copy(0, t).start()
            g_copy(1, t).start()

        def emit(t):
            g_copy(0, t, False).wait_recv()
            g_copy(2, t).start()
            g_copy(1, t, False).wait_recv()

        def emit_dot(t):
            g_copy(2, t, False).wait_recv()
            gated = gat[span(t), :]
            for d in range(2):
                acc[d, t] = lax.dot_general(
                    gated, w_out[section, d], (((1,), (1,)), ((), ())), preferred_element_type=F32
                )

                @pl.when(place[d] == 0)
                def _():
                    r_send[d, t] = acc[d, t].astype(BF)
                    r_copy(d, t).start()

            @pl.when(s > 0)
            def _():
                for d in range(2):
                    @pl.when((place[d] < last) & (place[d] > 0))
                    def _():
                        b_copy(d, t).wait_send()

                    @pl.when(place[d] == last)
                    def _():
                        b_copy(d, t).wait_send()

        def filtering(u):
            for lag, body in ((0, mix), (2, emit), (4, emit_dot)):
                @pl.when((u >= lag) & (u < CHUNKS + lag))
                def _():
                    body(u - lag)

        each(CHUNKS + 4, filtering)

        def settle(t):
            for slot in range(2):
                p_copy(slot, t).wait_send()
            for rel in range(3):
                ss_copy(rel, t).wait_send()
            x_copy(t).wait_send()
            for kind in range(3):
                g_copy(kind, t).wait_send()

        each(CHUNKS, settle)

        def chain(u):
            for d in range(2):
                t = u - (place[d] - 1) * SKEW
                inside = (t >= 0) & (t < CHUNKS)

                @pl.when(inside & (place[d] > 0) & (place[d] < last))
                def _():
                    r_copy(d, t).wait_recv()
                    r_send[d, t] = (acc[d, t] + r_recv[d, t].astype(F32)).astype(BF)
                    r_copy(d, t).start()

                @pl.when(inside & (place[d] == last))
                def _():
                    r_copy(d, t).wait_recv()
                    update = acc[d, t] + r_recv[d, t].astype(F32)
                    columns = pl.ds(d * half, half)
                    h[span(t), columns] = (h[span(t), columns].astype(F32) + update).astype(BF)
                    b_copy(d, t).start()

            for d in range(2):
                t = u - (2 + last - place[d]) * SKEW
                inside = (t >= 0) & (t < CHUNKS)

                @pl.when(inside & (place[d] > 0) & (place[d] < last))
                def _():
                    b_copy(d, t).wait_recv()
                    b_copy(d, t).start()

            @pl.when(s + 1 < STEPS)
            def _():
                entering(s + 1, u - ENTRY)

        each(jnp.where(s + 1 < STEPS, CHUNKS + 1 + ENTRY, CHUNKS + (2 * last - 2) * SKEW), chain)


        def settle_chain(t):
            for d in range(2):
                @pl.when(place[d] < last)
                def _():
                    r_copy(d, t).wait_send()

        each(CHUNKS, settle_chain)
        return carry

    each(CHUNKS + 1, partial(entering, 0))
    lax.fori_loop(0, STEPS, step, 0)
    each(CHUNKS, arrive)

    def finish(t):
        for d in range(2):
            @pl.when(place[d] > 0)
            def _():
                b_copy(d, t).wait_send()

    each(CHUNKS, finish)

    def out_copy(target):
        there = pl.ds(target * block_rows, block_rows)
        return remote(h.at[there, :], out, o_s.at[target], o_r, {"ctx": target})

    @pl.when(corner)
    def _():
        for target in range(n_ctx):
            @pl.when(ctx != target)
            def _():
                out_copy(target).start()
        keep = pltpu.make_async_copy(h.at[mine, :], out, local_sem)
        keep.start()
        keep.wait()
        for target in range(n_ctx):
            @pl.when(ctx != target)
            def _():
                out_copy(target).wait_send()

    @pl.when(jnp.logical_not(corner))
    def _():
        out_copy(0).wait_recv()


def stationary(stream, in_weights, out_weights, short_taps, medium_taps, plan):
    n_ctx = lax.axis_size("ctx")
    n_chan = lax.axis_size("chan")
    ctx = lax.axis_index("ctx")
    features, channels = in_weights.shape[1], in_weights.shape[3]
    tokens = stream.shape[0] * n_ctx
    rows = tokens // CHUNKS
    half = features // 2
    block = 3 * LANES
    reach = medium_taps.shape[0]
    w_in = in_weights.transpose(0, 2, 1, 3)
    w_out = out_weights.reshape(2, 2, half, channels)
    taps = jnp.stack([section_taps(section, short_taps, medium_taps) for section in range(2)])
    taps = lax.dynamic_slice_in_dim(taps, ctx * LANES, LANES, 2).astype(F32)
    taps = taps.reshape(2, reach // 8, 8, LANES)
    vmem = pl.BlockSpec(memory_space=pltpu.VMEM)
    dma = pltpu.SemaphoreType.DMA
    scratch = [
        pltpu.VMEM((tokens, features), BF),
        pltpu.VMEM((2, CHUNKS, rows, block), BF),
        pltpu.VMEM((2, CHUNKS, rows, block), BF),
        pltpu.VMEM((CHUNKS, rows, block), BF),
        pltpu.VMEM((CHUNKS, rows, block), BF),
        pltpu.VMEM((CHUNKS, rows, block), F32),
        pltpu.VMEM((CHUNKS, 8, rows), F32),
        pltpu.VMEM((3, CHUNKS, 8, rows), F32),
        pltpu.VMEM((PAD + tokens, LANES), F32),
        pltpu.VMEM((8, LANES), F32),
        pltpu.VMEM((tokens, channels), BF),
        pltpu.VMEM((2, CHUNKS, rows, half), F32),
        pltpu.VMEM((2, CHUNKS, rows, half), BF),
        pltpu.VMEM((2, CHUNKS, rows, half), BF),
        dma((n_chan,)), dma((n_ctx,)),
        dma((3, CHUNKS)), dma((3, CHUNKS)),
        dma((2, CHUNKS)), dma((2, CHUNKS)),
        dma((CHUNKS,)), dma((CHUNKS,)),
        dma((3, CHUNKS)), dma((3, CHUNKS)),
        dma((2, CHUNKS)), dma((2, CHUNKS)),
        dma((2, CHUNKS)), dma((2, CHUNKS)),
        dma((n_ctx,)), dma(()), dma(()),
    ]
    sizes = (tokens, rows, block, features * n_ctx, half)
    return pl.pallas_call(
        partial(stationary_kernel, sizes),
        out_shape=jax.ShapeDtypeStruct(stream.shape, stream.dtype),
        in_specs=[pl.BlockSpec(memory_space=pltpu.SMEM)] + [vmem] * 4,
        out_specs=vmem,
        scratch_shapes=scratch,
        compiler_params=pltpu.CompilerParams(
            collective_id=0, has_side_effects=True, vmem_limit_bytes=60 * 1024 * 1024
        ),
    )(plan, stream, w_in, w_out, taps)


def fits(mesh, stream, in_weights, medium_taps):
    n_ctx, n_chan = mesh.shape["ctx"], mesh.shape["chan"]
    tokens = stream.shape[0] // mesh.shape["groups"]
    channels = in_weights.shape[3] // n_chan
    return (
        n_ctx == 4 and n_chan == 4 and channels == n_ctx * LANES
        and stream.shape[1] // n_chan == in_weights.shape[1] // n_ctx
        and tokens % (CHUNKS * PAD) == 0 and medium_taps.shape[0] <= PAD
    )


def solution(mesh):
    def run(stream, in_weights, out_weights, short_taps, medium_taps, plan):
        body = stationary if fits(mesh, stream, in_weights, medium_taps) else shards
        return jax.shard_map(
            body,
            mesh=mesh,
            in_specs=(
                P(("groups", "ctx"), "chan"),
                P(None, "ctx", None, "chan"),
                P(None, "ctx", "chan"),
                P(None, "chan"),
                P(None, "chan"),
                P(),
            ),
            out_specs=P(("groups", "ctx"), "chan"),
            check_vma=False,
        )(stream, in_weights, out_weights, short_taps, medium_taps, plan)

    return run
```

profile of v0, /device:TPU:3, one launch (start us, length us, event | category | flops | bytes accessed | tf_op | source)
XLA Modules:
  0.0 299.3 jit_solution(7221047278002312992)
XLA Ops:
  0.0 0.9 copy.8
  0.9 0.7 broadcast_in_dim.2
  1.7 0.8 copy.9
  2.4 295.1 %shard_map.64 = bf16[192,1024]{1,0:T(8,128)(2,1)} custom-call(s32[4]{0:T(128)} %plan.1, bf16[192,1024]{1,0:T(8,128)(2,1)} %stream.1, bf16[2,3,1024,512]{3,2,1,0:T(8,128)(2,1)} %bitcast.6, bf16[2,2,512,512]{3,2,1,0:T(8,128)(2,1)} %bitcast.7, f32[2,16,8,128]{3,2,1,0:T(8,128)} %bitcast.8), custom_call_target="tpu_custom_call" | custom-call | tf_op jit(solution)/shard_map/pallas_call | solution.py:466
  297.5 1.8 copy.11
  (2 shorter events, 0.0 us)
where the time goes:
time: 300 us; the launch traced here: 299 us
  Pallas kernels  295 us (98%)
  local copies, waits for them, and re-layouts  4.14 us (1%)
    pallas_call x1, Pallas kernels, stationary(): pl.pallas_call(partial(stationary_kernel, sizes), out_shape=jax.ShapeDtyp...  295 us

commit v1 on v0

v1 whole, which is shorter than its diff:
```python
from functools import partial

import jax
import jax.numpy as jnp
from jax import lax
from jax.experimental import pallas as pl
from jax.experimental.pallas import tpu as pltpu
from jax.sharding import PartitionSpec as P

STEPS = 4


def passed_along(value, axis, steps):
    count = lax.axis_size(axis)
    leading, last = (max(0, -steps), min(count, count - steps))
    return lax.ppermute(value, axis, [(source, source + steps) for source in range(leading, last)])


def section_taps(section, short_taps, medium_taps):
    reach = medium_taps.shape[0]
    channels = short_taps.shape[1]
    padding = jnp.zeros((reach - short_taps.shape[0], channels), short_taps.dtype)
    short_full = jnp.concatenate([short_taps, padding], 0)
    group_size = channels // medium_taps.shape[1]
    medium_full = jnp.broadcast_to(
        medium_taps[:, :, None], (reach, medium_taps.shape[1], group_size)
    ).reshape(reach, channels)
    return jnp.where(section == 0, short_full, medium_full)


def causal_filter(extended, filter_taps):
    filtered = lax.conv_general_dilated(
        extended[None],
        filter_taps[::-1][:, None, :],
        (1,),
        "VALID",
        dimension_numbers=("NWC", "WIO", "NWC"),
        feature_group_count=filter_taps.shape[1],
        preferred_element_type=jnp.float32,
    )
    return filtered[0]


def filter_gate(projected, section, short_taps, medium_taps):
    query_bf = projected[:, 0].astype(jnp.bfloat16)
    mixed_bf = (projected[:, 1] * projected[:, 2]).astype(jnp.bfloat16)
    reach = medium_taps.shape[0]
    earlier = passed_along(mixed_bf[-reach:], "ctx", 1)
    extended = jnp.concatenate([earlier[1:], mixed_bf], 0)
    filtered = causal_filter(extended, section_taps(section, short_taps, medium_taps))
    return (query_bf.astype(jnp.float32) * filtered).astype(jnp.bfloat16)


def expand_rows(hidden):
    return lax.all_gather(hidden, "chan", axis=1, tiled=True)


def combine(hidden, partial_sum):
    update = lax.psum_scatter(
        partial_sum.astype(jnp.bfloat16), "chan", scatter_dimension=1, tiled=True
    ).astype(jnp.float32)
    return (hidden.astype(jnp.float32) + update).astype(jnp.bfloat16)


def advance(hidden, section, project, emit, short_taps, medium_taps):
    full_rows = expand_rows(hidden)
    widened = full_rows.astype(jnp.float32)
    row_scale = lax.rsqrt(jnp.mean(widened * widened, axis=1, keepdims=True) + 1e-05)
    projected, kept_in = project(full_rows, section)
    projected = projected.reshape(full_rows.shape[0], 3, -1) * row_scale[:, :, None]
    gated_bf = filter_gate(projected, section, short_taps, medium_taps)
    partial_sum, kept_out = emit(gated_bf, section)
    return (combine(hidden, partial_sum), kept_in, kept_out)


def stored_project(weights_in, full_rows, section):
    chosen = lax.dynamic_index_in_dim(weights_in, section, 0, keepdims=False)
    projected = jnp.dot(
        full_rows, chosen.reshape(chosen.shape[0], -1), preferred_element_type=jnp.float32
    )
    return (projected, weights_in)


def stored_emit(weights_out, gated_bf, section):
    chosen = lax.dynamic_index_in_dim(weights_out, section, 0, keepdims=False)
    product = lax.dot_general(
        gated_bf, chosen, (((1,), (1,)), ((), ())), preferred_element_type=jnp.float32
    )
    return (product, weights_out)


def shards(stream, in_weights, out_weights, short_taps, medium_taps, plan):
    hidden = stream
    weights_in, weights_out = (
        lax.all_gather(in_weights, "ctx", axis=1, tiled=True),
        lax.all_gather(out_weights, "ctx", axis=1, tiled=True),
    )
    first_step = 0
    for step_index in range(first_step, STEPS):
        hidden, weights_in, weights_out = advance(
            hidden,
            plan[step_index],
            partial(stored_project, weights_in),
            partial(stored_emit, weights_out),
            short_taps,
            medium_taps,
        )
    return hidden


CHUNKS = 12
CROSS, MIX, EMIT, DOT, MEET, UPDATE, ARRIVE = 1, 3, 4, 5, 7, 9, 12
PAD = 128
LANES = 128
BF = jnp.bfloat16
F32 = jnp.float32


def wave_kernel(
    sizes, plan, stream, w_in, w_out, taps, out,
    h, land, p_send, p_recv, x_send, x_recv, own, ss_own, ss_recv, mixed, gat, acc, r_send, r_recv, c_recv,
    i_r, up_s, down_s, m_s, m_r, ss_s, ss_r, p_s, p_r, x_s, x_r, g_s, g_r, r_s, r_r, c_s, c_r, b_s, b_r, o_s, o_r,
):
    tokens, rows, block, width = sizes
    ctx, chan = lax.axis_index("ctx"), lax.axis_index("chan")
    n_ctx, n_chan = 4, 4
    side, core = ctx // 2, ctx % 2
    partner = {"ctx": side * 2 + (1 - core)}
    across = {"ctx": (1 - side) * 2 + core}
    diagonal = {"ctx": (1 - side) * 2 + (1 - core)}
    relations = (partner, across, diagonal)
    last = n_chan - 1
    outer = (chan == 0) | (chan == last)
    inner = jnp.logical_not(outer)
    near = {"chan": chan + 1 - 2 * (chan % 2)}
    mid = {"chan": jnp.where(outer, near["chan"], last - chan)}
    above = {"chan": jnp.minimum(chan + 1, last)}
    below = {"chan": jnp.maximum(chan - 1, 0)}
    corner = ctx == chan
    items = STEPS * CHUNKS
    each_block = CHUNKS // n_ctx

    def remote(source, target, send, recv, device):
        return pltpu.make_async_remote_copy(
            src_ref=source, dst_ref=target, send_sem=send, recv_sem=recv,
            device_id=device, device_id_type=pl.DeviceIdType.MESH,
        )

    def span(t):
        return pl.ds(pl.multiple_of(t * rows, rows), rows)

    def lanes(index):
        return pl.ds(pl.multiple_of(index * LANES, LANES), LANES)

    def each(count, body):
        def wrapped(t, carry):
            body(t)
            return carry
        lax.fori_loop(0, count, wrapped, 0)

    barrier = pltpu.get_barrier_semaphore()
    for di in range(n_ctx):
        for dk in range(n_chan):
            if di or dk:
                pl.semaphore_signal(
                    barrier, inc=1,
                    device_id={"ctx": (ctx + di) % n_ctx, "chan": (chan + dk) % n_chan},
                    device_id_type=pl.DeviceIdType.MESH,
                )
    pl.semaphore_wait(barrier, n_ctx * n_chan - 1)

    def hop_copy(source, q, j, upward):
        sems, device = (up_s, above) if upward else (down_s, below)
        return remote(source, land.at[q, span(j), :], sems.at[q, j], i_r.at[q, j], device)

    def spread_copy(source, q, j):
        chunk = ctx * each_block + j
        return remote(source, h.at[span(chunk), :], m_s.at[q, j], m_r.at[chunk], {"ctx": q})

    def keep_copy(source, j):
        chunk = ctx * each_block + j
        return pltpu.make_async_copy(source, h.at[span(chunk), :], m_r.at[chunk])

    def spread(source, q, j):
        @pl.when(q != ctx)
        def _():
            spread_copy(source, q, j).start()

        @pl.when(q == ctx)
        def _():
            keep_copy(source, j).start()

    def first(j):
        source = stream.at[span(j), :]

        @pl.when(chan < last)
        def _():
            hop_copy(source, chan, j, True).start()

        @pl.when(chan > 0)
        def _():
            hop_copy(source, chan, j, False).start()

        spread(source, chan, j)

    def relay(j):
        for distance in range(1, n_chan):
            @pl.when(chan >= distance)
            def _():
                q = chan - distance
                source = land.at[q, span(j), :]
                hop_copy(source, q, j, True).wait_recv()

                @pl.when(chan < last)
                def _():
                    hop_copy(source, q, j, True).start()

                spread(source, q, j)

            @pl.when(chan + distance <= last)
            def _():
                q = chan + distance
                source = land.at[q, span(j), :]
                hop_copy(source, q, j, False).wait_recv()

                @pl.when(chan > 0)
                def _():
                    hop_copy(source, q, j, False).start()

                spread(source, q, j)

    def relay_settle(j):
        for q in range(n_chan):
            source = land.at[q, span(j), :]

            @pl.when((q <= chan) & (chan < last))
            def _():
                hop_copy(source, q, j, True).wait_send()

            @pl.when((q >= chan) & (chan > 0))
            def _():
                hop_copy(source, q, j, False).wait_send()

            @pl.when(q != ctx)
            def _():
                spread_copy(source, q, j).wait_send()

    def first_arrive(t):
        @pl.when(t // each_block == ctx)
        def _():
            pltpu.make_async_copy(stream.at[span(0), :], h.at[span(t), :], m_r.at[t]).wait()

        @pl.when(t // each_block != ctx)
        def _():
            remote(stream.at[span(0), :], h.at[span(t), :], m_s.at[0, 0], m_r.at[t], partner).wait_recv()

    def ss_copy(rel, t):
        return remote(ss_own.at[t], ss_recv.at[rel, t], ss_s.at[rel, t], ss_r.at[rel, t], relations[rel])

    def p_copy(slot, t):
        return remote(p_send.at[slot, t], p_recv.at[slot, t], p_s.at[slot, t], p_r.at[slot, t], partner)

    def x_copy(t):
        return remote(x_send.at[t], x_recv.at[t], x_s.at[t], x_r.at[t], across)

    def g_copy(kind, t, sending=True):
        owner = (1 - side) * 2 + core if kind == 2 else ctx
        if not sending:
            owner = (across["ctx"], partner["ctx"], diagonal["ctx"])[kind]
        ref = gat.at[span(t), lanes(owner)]
        return remote(ref, ref, g_s.at[kind, t], g_r.at[kind, t], across if kind == 0 else partner)

    def r_copy(t):
        return remote(r_send.at[t], r_recv.at[t], r_s.at[t], r_r.at[t], near)

    def c_copy(parity, t):
        return remote(r_send.at[t], c_recv.at[parity, t], c_s.at[parity, t], c_r.at[parity, t], mid)

    def b_copy(t):
        ref = h.at[span(t), :]
        return remote(ref, ref, b_s.at[t], b_r.at[t], near)

    home = side == chan // 2

    def gives(s):
        return inner & ((s + 1 < STEPS) | jnp.logical_not(home))

    def takes(s):
        return inner & ((s + 1 < STEPS) | home)

    def returns(s):
        return inner & ((s + 1 < STEPS) | (ctx == near["chan"]))

    def awaits(s):
        return outer & ((s + 1 < STEPS) | corner)

    def settle(s, t):
        for slot in range(2):
            p_copy(slot, t).wait_send()
        for rel in range(3):
            ss_copy(rel, t).wait_send()
        x_copy(t).wait_send()
        for kind in range(3):
            g_copy(kind, t).wait_send()

        @pl.when(outer)
        def _():
            r_copy(t).wait_send()

        @pl.when(gives(s))
        def _():
            c_copy(s % 2, t).wait_send()

        @pl.when(returns(s))
        def _():
            b_copy(t).wait_send()

    def project(section, t, index):
        columns = lanes(index)
        weights = jnp.concatenate([w_in[section, j, :, columns] for j in range(3)], 1)
        return jnp.dot(h[span(t), :], weights, preferred_element_type=F32)

    def enter(s, t):
        section = plan[s]

        @pl.when(s > 0)
        def _():
            settle(s - 1, t)

            @pl.when(outer)
            def _():
                b_copy(t).wait_recv()

        @pl.when(s == 0)
        def _():
            first_arrive(t)

        p_send[0, t] = project(section, t, diagonal["ctx"]).astype(BF)
        p_copy(0, t).start()
        p_send[1, t] = project(section, t, partner["ctx"]).astype(BF)
        p_copy(1, t).start()
        wide = h[span(t), :].astype(F32)
        squares = (wide * wide).astype(BF)
        ss_own[t, :, pl.ds(0, rows)] = lax.dot_general(
            jnp.ones((8, squares.shape[1]), BF), squares, (((1,), (1,)), ((), ())), preferred_element_type=F32
        )
        for rel in range(3):
            ss_copy(rel, t).start()

    def cross(s, t):
        section = plan[s]
        passing = project(section, t, across["ctx"])
        p_copy(0, t).wait_recv()
        x_send[t] = (passing + p_recv[0, t].astype(F32)).astype(BF)
        x_copy(t).start()
        own[t] = project(section, t, ctx)

    def mix(s, t):
        section = plan[s]
        for rel in range(3):
            ss_copy(rel, t).wait_recv()
        p_copy(1, t).wait_recv()
        x_copy(t).wait_recv()
        total = ss_own[t] + ss_recv[0, t] + ss_recv[1, t] + ss_recv[2, t]
        scale = lax.rsqrt(total * (1.0 / width) + 1e-05)
        scale = jnp.transpose(scale)[:rows, :1]
        parts = (own[t] + p_recv[1, t].astype(F32) + x_recv[t].astype(F32)) * scale
        query = parts[:, :LANES].astype(BF).astype(F32)
        product = parts[:, LANES:2 * LANES] * parts[:, 2 * LANES:]
        mixed[pl.ds(pl.multiple_of(PAD + t * rows, rows), rows), :] = product.astype(BF).astype(F32)

        def tap_block(jj, total):
            start = pl.multiple_of(PAD + t * rows - 8 * jj - 8, 8)
            window = mixed[pl.ds(start, rows + 8), :]
            weights = taps[section, jj]
            for c in range(8):
                total = total + weights[c:c + 1, :] * window[8 - c:8 - c + rows, :]
            return total

        filtered = lax.fori_loop(0, taps.shape[1], tap_block, jnp.zeros((rows, LANES), F32))
        gat[span(t), lanes(ctx)] = (query * filtered).astype(BF)
        g_copy(0, t).start()
        g_copy(1, t).start()

    def emit(s, t):
        g_copy(0, t, False).wait_recv()
        g_copy(2, t).start()

    def dot(s, t):
        section = plan[s]
        g_copy(1, t, False).wait_recv()
        g_copy(2, t, False).wait_recv()
        product = lax.dot_general(
            gat[span(t), :], w_out[section], (((1,), (1,)), ((), ())), preferred_element_type=F32
        )

        @pl.when(outer)
        def _():
            r_send[t] = product.astype(BF)
            r_copy(t).start()

        @pl.when(inner)
        def _():
            acc[t] = product

    def meet(s, t):
        @pl.when(inner)
        def _():
            r_copy(t).wait_recv()
            r_send[t] = (acc[t] + r_recv[t].astype(F32)).astype(BF)

        @pl.when(gives(s))
        def _():
            c_copy(s % 2, t).start()

    def update(s, t):
        @pl.when(takes(s))
        def _():
            parity = s % 2
            c_copy(parity, t).wait_recv()
            total = r_send[t].astype(F32) + c_recv[parity, t].astype(F32)
            h[span(t), :] = (h[span(t), :].astype(F32) + total).astype(BF)

        @pl.when(returns(s))
        def _():
            b_copy(t).start()

    def out_copy(t):
        there = span(t % each_block)
        return remote(h.at[span(t), :], out.at[there, :], o_s.at[t], o_r.at[t % each_block], {"ctx": t // each_block})

    def keep_out(t):
        there = span(t % each_block)
        return pltpu.make_async_copy(h.at[span(t), :], out.at[there, :], o_s.at[t])

    def leave(s, t):
        @pl.when((s + 1 == STEPS) & corner)
        def _():
            @pl.when(outer)
            def _():
                b_copy(t).wait_recv()

            @pl.when(t // each_block != ctx)
            def _():
                out_copy(t).start()

            @pl.when(t // each_block == ctx)
            def _():
                keep_out(t).start()

    stages = (
        (ARRIVE, leave), (UPDATE, update), (MEET, meet), (DOT, dot), (EMIT, emit), (MIX, mix), (CROSS, cross), (0, enter),
    )

    def tick(u):
        @pl.when(u < each_block)
        def _():
            relay(u)

        for lag, body in stages:
            @pl.when((u >= lag) & (u < items + lag))
            def _():
                n = u - lag
                body(n // CHUNKS, n % CHUNKS)

    mixed[pl.ds(0, PAD), :] = jnp.zeros((PAD, LANES), F32)
    ss_own[...] = jnp.zeros(ss_own.shape, F32)
    each(each_block, first)
    each(items + ARRIVE, tick)

    def finish(t):
        settle(STEPS - 1, t)

        @pl.when(corner & (t // each_block != ctx))
        def _():
            out_copy(t).wait_send()

        @pl.when(corner & (t // each_block == ctx))
        def _():
            keep_out(t).wait()

    each(CHUNKS, finish)

    def received(j):
        relay_settle(j)

        @pl.when(jnp.logical_not(corner))
        def _():
            out_copy(j).wait_recv()

    each(each_block, received)


def wave(stream, in_weights, out_weights, short_taps, medium_taps, plan):
    n_ctx = lax.axis_size("ctx")
    n_chan = lax.axis_size("chan")
    ctx = lax.axis_index("ctx")
    features, channels = in_weights.shape[1], in_weights.shape[3]
    tokens = stream.shape[0] * n_ctx
    rows = tokens // CHUNKS
    each_block = CHUNKS // n_ctx
    block = 3 * LANES
    reach = medium_taps.shape[0]
    w_in = in_weights.transpose(0, 2, 1, 3)
    taps = jnp.stack([section_taps(section, short_taps, medium_taps) for section in range(2)])
    taps = lax.dynamic_slice_in_dim(taps, ctx * LANES, LANES, 2).astype(F32)
    taps = taps.reshape(2, reach // 8, 8, LANES)
    vmem = pl.BlockSpec(memory_space=pltpu.VMEM)
    dma = pltpu.SemaphoreType.DMA
    scratch = [
        pltpu.VMEM((tokens, features), BF),
        pltpu.VMEM((n_chan, stream.shape[0], features), BF),
        pltpu.VMEM((2, CHUNKS, rows, block), BF),
        pltpu.VMEM((2, CHUNKS, rows, block), BF),
        pltpu.VMEM((CHUNKS, rows, block), BF),
        pltpu.VMEM((CHUNKS, rows, block), BF),
        pltpu.VMEM((CHUNKS, rows, block), F32),
        pltpu.VMEM((CHUNKS, 8, LANES), F32),
        pltpu.VMEM((3, CHUNKS, 8, LANES), F32),
        pltpu.VMEM((PAD + tokens, LANES), F32),
        pltpu.VMEM((tokens, channels), BF),
        pltpu.VMEM((CHUNKS, rows, features), F32),
        pltpu.VMEM((CHUNKS, rows, features), BF),
        pltpu.VMEM((CHUNKS, rows, features), BF),
        pltpu.VMEM((2, CHUNKS, rows, features), BF),
        dma((n_chan, each_block)), dma((n_chan, each_block)), dma((n_chan, each_block)),
        dma((n_chan, each_block)), dma((CHUNKS,)),
        dma((3, CHUNKS)), dma((3, CHUNKS)),
        dma((2, CHUNKS)), dma((2, CHUNKS)),
        dma((CHUNKS,)), dma((CHUNKS,)),
        dma((3, CHUNKS)), dma((3, CHUNKS)),
        dma((CHUNKS,)), dma((CHUNKS,)),
        dma((2, CHUNKS)), dma((2, CHUNKS)),
        dma((CHUNKS,)), dma((CHUNKS,)),
        dma((CHUNKS,)), dma((each_block,)),
    ]
    sizes = (tokens, rows, block, features * n_ctx)
    return pl.pallas_call(
        partial(wave_kernel, sizes),
        out_shape=jax.ShapeDtypeStruct(stream.shape, stream.dtype),
        in_specs=[pl.BlockSpec(memory_space=pltpu.SMEM)] + [vmem] * 4,
        out_specs=vmem,
        scratch_shapes=scratch,
        compiler_params=pltpu.CompilerParams(
            collective_id=0, has_side_effects=True, vmem_limit_bytes=60 * 1024 * 1024
        ),
    )(plan, stream, w_in, out_weights, taps)


def fits(mesh, stream, in_weights, medium_taps):
    n_ctx, n_chan = mesh.shape["ctx"], mesh.shape["chan"]
    tokens = stream.shape[0] // mesh.shape["groups"]
    channels = in_weights.shape[3] // n_chan
    return (
        n_ctx == 4 and n_chan == 4 and channels == n_ctx * LANES
        and stream.shape[1] // n_chan == in_weights.shape[1] // n_ctx
        and tokens == 768 and medium_taps.shape[0] == PAD
    )


def solution(mesh):
    def run(stream, in_weights, out_weights, short_taps, medium_taps, plan):
        body = wave if fits(mesh, stream, in_weights, medium_taps) else shards
        return jax.shard_map(
            body,
            mesh=mesh,
            in_specs=(
                P(("groups", "ctx"), "chan"),
                P(None, "ctx", None, "chan"),
                P(None, "ctx", "chan"),
                P(None, "chan"),
                P(None, "chan"),
                P(),
            ),
            out_specs=P(("groups", "ctx"), "chan"),
            check_vma=False,
        )(stream, in_weights, out_weights, short_taps, medium_taps, plan)

    return run
```

time: 300 us -> 237 us (0.79)
  Pallas kernels: 295 us -> 232 us
    pallas_call x1, Pallas kernels: 295 us -> 232 us  [wave(): pl.pallas_call(partial(wave_kernel, sizes), out_shape=jax.ShapeDtypeStruc...]
where the time goes in v1:
time: 237 us; the launch traced here: 236 us
  Pallas kernels  232 us (98%)
  local copies, waits for them, and re-layouts  4.14 us (2%)
    pallas_call x1, Pallas kernels, wave(): pl.pallas_call(partial(wave_kernel, sizes), out_shape=jax.ShapeDtypeStruc...  232 us

profile of v1, /device:TPU:3, one launch (start us, length us, event | category | flops | bytes accessed | tf_op | source)
XLA Modules:
  0.0 235.9 jit_solution(12456402190383603817)
XLA Ops:
  0.0 0.9 copy.8
  0.9 0.7 broadcast_in_dim.2
  1.7 0.8 copy.9
  2.4 231.8 %shard_map.64 = bf16[192,1024]{1,0:T(8,128)(2,1)} custom-call(s32[4]{0:T(128)} %plan.1, bf16[192,1024]{1,0:T(8,128)(2,1)} %stream.1, bf16[2,3,1024,512]{3,2,1,0:T(8,128)(2,1)} %bitcast.5, bf16[2,1024,512]{2,1,0:T(8,128)(2,1)} %w_out.1, f32[2,16,8,128]{3,2,1,0:T(8,128)} %bitcast.6), custom_call_target="tpu_custom_call" | custom-call | tf_op jit(solution)/shard_map/pallas_call | solution.py:538
  234.2 1.8 copy.11
  (2 shorter events, 0.1 us)

commit v2 on v1

--- a/solution.py
+++ b/solution.py
@@ -109,7 +109,7 @@
 
 
 CHUNKS = 12
-CROSS, MIX, EMIT, DOT, MEET, UPDATE, ARRIVE = 1, 3, 4, 5, 7, 9, 12
+CROSS, MIX, DOT, MEET, UPDATE, ARRIVE = 1, 3, 5, 7, 9, 12
 PAD = 128
 LANES = 128
 BF = jnp.bfloat16
@@ -117,9 +117,9 @@
 
 
 def wave_kernel(
-    sizes, plan, stream, w_in, w_out, taps, out,
-    h, land, p_send, p_recv, x_send, x_recv, own, ss_own, ss_recv, mixed, gat, acc, r_send, r_recv, c_recv,
-    i_r, up_s, down_s, m_s, m_r, ss_s, ss_r, p_s, p_r, x_s, x_r, g_s, g_r, r_s, r_r, c_s, c_r, b_s, b_r, o_s, o_r,
+    sizes, plan, stream, w_in_hbm, w_out_hbm, short_taps, medium_taps, out,
+    h, w_in, w_out, taps, land, p_send, p_recv, x_send, x_recv, own, ss_own, ss_recv, mixed, gat, acc, r_send, r_recv, c_recv,
+    i_r, up_s, down_s, m_s, m_r, ss_s, ss_r, p_s, p_r, x_s, x_r, g_s, g_r, r_s, r_r, c_s, c_r, b_s, b_r, o_s, o_r, w_s,
 ):
     tokens, rows, block, width = sizes
     ctx, chan = lax.axis_index("ctx"), lax.axis_index("chan")
@@ -167,6 +167,8 @@
                     device_id={"ctx": (ctx + di) % n_ctx, "chan": (chan + dk) % n_chan},
                     device_id_type=pl.DeviceIdType.MESH,
                 )
+    in_load = pltpu.make_async_copy(w_in_hbm, w_in, w_s.at[0])
+    out_load = pltpu.make_async_copy(w_out_hbm, w_out, w_s.at[1])
     pl.semaphore_wait(barrier, n_ctx * n_chan - 1)
 
     def hop_copy(source, q, j, upward):
@@ -263,12 +265,9 @@
     def x_copy(t):
         return remote(x_send.at[t], x_recv.at[t], x_s.at[t], x_r.at[t], across)
 
-    def g_copy(kind, t, sending=True):
-        owner = (1 - side) * 2 + core if kind == 2 else ctx
-        if not sending:
-            owner = (across["ctx"], partner["ctx"], diagonal["ctx"])[kind]
-        ref = gat.at[span(t), lanes(owner)]
-        return remote(ref, ref, g_s.at[kind, t], g_r.at[kind, t], across if kind == 0 else partner)
+    def g_copy(rel, t, sending=True):
+        ref = gat.at[span(t), lanes(ctx if sending else relations[rel]["ctx"])]
+        return remote(ref, ref, g_s.at[rel, t], g_r.at[rel, t], relations[rel])
 
     def r_copy(t):
         return remote(r_send.at[t], r_recv.at[t], r_s.at[t], r_r.at[t], near)
@@ -367,29 +366,28 @@
         parts = (own[t] + p_recv[1, t].astype(F32) + x_recv[t].astype(F32)) * scale
         query = parts[:, :LANES].astype(BF).astype(F32)
         product = parts[:, LANES:2 * LANES] * parts[:, 2 * LANES:]
-        mixed[pl.ds(pl.multiple_of(PAD + t * rows, rows), rows), :] = product.astype(BF).astype(F32)
+        base = PAD + t * rows
+        before = mixed[0, pl.ds(pl.multiple_of(base - 8, 8), 8), :]
+        window = jnp.concatenate([before, product.astype(BF).astype(F32)], 0)
+        for c in range(8):
+            mixed[c, pl.ds(pl.multiple_of(base, rows), rows), :] = window[8 - c:8 - c + rows, :]
 
         def tap_block(jj, total):
-            start = pl.multiple_of(PAD + t * rows - 8 * jj - 8, 8)
-            window = mixed[pl.ds(start, rows + 8), :]
+            here = pl.ds(pl.multiple_of(base - 8 * jj, 8), rows)
             weights = taps[section, jj]
             for c in range(8):
-                total = total + weights[c:c + 1, :] * window[8 - c:8 - c + rows, :]
+                total = total + weights[c:c + 1, :] * mixed[c, here, :]
             return total
 
         filtered = lax.fori_loop(0, taps.shape[1], tap_block, jnp.zeros((rows, LANES), F32))
         gat[span(t), lanes(ctx)] = (query * filtered).astype(BF)
-        g_copy(0, t).start()
-        g_copy(1, t).start()
-
-    def emit(s, t):
-        g_copy(0, t, False).wait_recv()
-        g_copy(2, t).start()
+        for rel in (2, 1, 0):
+            g_copy(rel, t).start()
 
     def dot(s, t):
         section = plan[s]
-        g_copy(1, t, False).wait_recv()
-        g_copy(2, t, False).wait_recv()
+        for rel in range(3):
+            g_copy(rel, t, False).wait_recv()
         product = lax.dot_general(
             gat[span(t), :], w_out[section], (((1,), (1,)), ((), ())), preferred_element_type=F32
         )
@@ -449,7 +447,7 @@
                 keep_out(t).start()
 
     stages = (
-        (ARRIVE, leave), (UPDATE, update), (MEET, meet), (DOT, dot), (EMIT, emit), (MIX, mix), (CROSS, cross), (0, enter),
+        (ARRIVE, leave), (UPDATE, update), (MEET, meet), (DOT, dot), (MIX, mix), (CROSS, cross), (0, enter),
     )
 
     def tick(u):
@@ -463,9 +461,26 @@
                 n = u - lag
                 body(n // CHUNKS, n % CHUNKS)
 
-    mixed[pl.ds(0, PAD), :] = jnp.zeros((PAD, LANES), F32)
+    each(each_block, first)
+    in_load.start()
+    out_load.start()
+    for c in range(8):
+        mixed[c, pl.ds(0, PAD), :] = jnp.zeros((PAD, LANES), F32)
     ss_own[...] = jnp.zeros(ss_own.shape, F32)
-    each(each_block, first)
+    groups, reach = medium_taps.shape
+    share = LANES // (groups // n_ctx)
+    row = lax.broadcasted_iota(jnp.int32, (groups, LANES), 0)
+    lane = lax.broadcasted_iota(jnp.int32, (groups, LANES), 1)
+    chosen = jnp.where(row == ctx * (groups // n_ctx) + lane // share, 1.0, 0.0).astype(BF)
+    spread_taps = lax.dot_general(
+        medium_taps[...], chosen, (((0,), (0,)), ((), ())), preferred_element_type=F32
+    )
+    taps[1] = spread_taps.reshape(reach // 8, 8, LANES)
+    taps[0] = jnp.zeros((reach // 8, 8, LANES), F32)
+    count = short_taps.shape[0]
+    taps[0, 0, pl.ds(0, count), :] = short_taps[:, lanes(ctx)].astype(F32)
+    in_load.wait()
+    out_load.wait()
     each(items + ARRIVE, tick)
 
     def finish(t):
@@ -494,7 +509,6 @@
 def wave(stream, in_weights, out_weights, short_taps, medium_taps, plan):
     n_ctx = lax.axis_size("ctx")
     n_chan = lax.axis_size("chan")
-    ctx = lax.axis_index("ctx")
     features, channels = in_weights.shape[1], in_weights.shape[3]
     tokens = stream.shape[0] * n_ctx
     rows = tokens // CHUNKS
@@ -502,13 +516,14 @@
     block = 3 * LANES
     reach = medium_taps.shape[0]
     w_in = in_weights.transpose(0, 2, 1, 3)
-    taps = jnp.stack([section_taps(section, short_taps, medium_taps) for section in range(2)])
-    taps = lax.dynamic_slice_in_dim(taps, ctx * LANES, LANES, 2).astype(F32)
-    taps = taps.reshape(2, reach // 8, 8, LANES)
     vmem = pl.BlockSpec(memory_space=pltpu.VMEM)
+    anywhere = pl.BlockSpec(memory_space=pl.ANY)
     dma = pltpu.SemaphoreType.DMA
     scratch = [
         pltpu.VMEM((tokens, features), BF),
+        pltpu.VMEM(w_in.shape, BF),
+        pltpu.VMEM(out_weights.shape, BF),
+        pltpu.VMEM((2, reach // 8, 8, LANES), F32),
         pltpu.VMEM((n_chan, stream.shape[0], features), BF),
         pltpu.VMEM((2, CHUNKS, rows, block), BF),
         pltpu.VMEM((2, CHUNKS, rows, block), BF),
@@ -517,7 +532,7 @@
         pltpu.VMEM((CHUNKS, rows, block), F32),
         pltpu.VMEM((CHUNKS, 8, LANES), F32),
         pltpu.VMEM((3, CHUNKS, 8, LANES), F32),
-        pltpu.VMEM((PAD + tokens, LANES), F32),
+        pltpu.VMEM((8, PAD + tokens, LANES), F32),
         pltpu.VMEM((tokens, channels), BF),
         pltpu.VMEM((CHUNKS, rows, features), F32),
         pltpu.VMEM((CHUNKS, rows, features), BF),
@@ -532,19 +547,19 @@
         dma((CHUNKS,)), dma((CHUNKS,)),
         dma((2, CHUNKS)), dma((2, CHUNKS)),
         dma((CHUNKS,)), dma((CHUNKS,)),
-        dma((CHUNKS,)), dma((each_block,)),
+        dma((CHUNKS,)), dma((each_block,)), dma((2,)),
     ]
     sizes = (tokens, rows, block, features * n_ctx)
     return pl.pallas_call(
         partial(wave_kernel, sizes),
         out_shape=jax.ShapeDtypeStruct(stream.shape, stream.dtype),
-        in_specs=[pl.BlockSpec(memory_space=pltpu.SMEM)] + [vmem] * 4,
+        in_specs=[pl.BlockSpec(memory_space=pltpu.SMEM), vmem, anywhere, anywhere, vmem, vmem],
         out_specs=vmem,
         scratch_shapes=scratch,
         compiler_params=pltpu.CompilerParams(
             collective_id=0, has_side_effects=True, vmem_limit_bytes=60 * 1024 * 1024
         ),
-    )(plan, stream, w_in, out_weights, taps)
+    )(plan, stream, w_in, out_weights, short_taps, medium_taps.T)
 
 
 def fits(mesh, stream, in_weights, medium_taps):

time: 237 us -> 200 us (0.84)
  Pallas kernels: 232 us -> 197 us
    pallas_call x1, Pallas kernels: 232 us -> 197 us  [wave(): pl.pallas_call(partial(wave_kernel, sizes), out_shape=jax.ShapeDtypeStruc...]
where the time goes in v2:
time: 200 us; the launch traced here: 199 us
  Pallas kernels  197 us (98%)
    pallas_call x1, Pallas kernels, wave(): pl.pallas_call(partial(wave_kernel, sizes), out_shape=jax.ShapeDtypeStruc...  197 us

profile of v2, /device:TPU:3, one launch (start us, length us, event | category | flops | bytes accessed | tf_op | source)
XLA Modules:
  0.0 198.9 jit_solution(11114848091236146242)
XLA Ops:
  0.0 197.2 %shard_map.64 = bf16[192,1024]{1,0:T(8,128)(2,1)} custom-call(s32[4]{0:T(128)} %plan.1, bf16[192,1024]{1,0:T(8,128)(2,1)} %stream.1, bf16[2,3,1024,512]{3,2,1,0:T(8,128)(2,1)} %bitcast.2, bf16[2,1024,512]{2,1,0:T(8,128)(2,1)} %w_out_hbm.1, bf16[7,512]{1,0:T(8,128)(2,1)} %short_taps.1, bf16[32,128]{1,0:T(8,128)(2,1)} %bitcast.3), custom_call_target="tpu_custom_call" | custom-call | tf_op jit(solution)/shard_map/pallas_call | solution.py:553
  197.2 1.8 copy.8

commit v3 on v2

--- a/solution.py
+++ b/solution.py
@@ -109,7 +109,7 @@
 
 
 CHUNKS = 12
-CROSS, MIX, DOT, MEET, UPDATE, ARRIVE = 1, 3, 5, 7, 9, 12
+CROSS, MIX, DOT, MEET, UPDATE = 1, 3, 5, 7, 9
 PAD = 128
 LANES = 128
 BF = jnp.bfloat16
@@ -117,7 +117,7 @@
 
 
 def wave_kernel(
-    sizes, plan, stream, w_in_hbm, w_out_hbm, short_taps, medium_taps, out,
+    sizes, plan, stream_hbm, w_in_hbm, w_out_hbm, short_taps, medium_taps, out,
     h, w_in, w_out, taps, land, p_send, p_recv, x_send, x_recv, own, ss_own, ss_recv, mixed, gat, acc, r_send, r_recv, c_recv,
     i_r, up_s, down_s, m_s, m_r, ss_s, ss_r, p_s, p_r, x_s, x_r, g_s, g_r, r_s, r_r, c_s, c_r, b_s, b_r, o_s, o_r, w_s,
 ):
@@ -159,17 +159,49 @@
         lax.fori_loop(0, count, wrapped, 0)
 
     barrier = pltpu.get_barrier_semaphore()
-    for di in range(n_ctx):
-        for dk in range(n_chan):
-            if di or dk:
-                pl.semaphore_signal(
-                    barrier, inc=1,
-                    device_id={"ctx": (ctx + di) % n_ctx, "chan": (chan + dk) % n_chan},
-                    device_id_type=pl.DeviceIdType.MESH,
-                )
+
+    def greet(**device):
+        pl.semaphore_signal(barrier, inc=1, device_id=device, device_id_type=pl.DeviceIdType.MESH)
+
+    for di in range(1, n_ctx):
+        greet(ctx=(ctx + di) % n_ctx, chan=chan)
+
+    @pl.when(chan < last)
+    def _():
+        greet(ctx=ctx, chan=chan + 1)
+
+    @pl.when(chan > 0)
+    def _():
+        greet(ctx=ctx, chan=chan - 1)
+
+    @pl.when(outer & (ctx != chan))
+    def _():
+        greet(ctx=chan, chan=near["chan"])
+
+    guests = n_ctx - 1 + jnp.where(outer, 1, 2) + jnp.where(inner & (ctx == near["chan"]), n_ctx - 1, 0)
+    own_load = pltpu.make_async_copy(stream_hbm, land.at[chan], w_s.at[2])
+    own_load.start()
     in_load = pltpu.make_async_copy(w_in_hbm, w_in, w_s.at[0])
     out_load = pltpu.make_async_copy(w_out_hbm, w_out, w_s.at[1])
-    pl.semaphore_wait(barrier, n_ctx * n_chan - 1)
+    in_load.start()
+    out_load.start()
+    for c in range(8):
+        mixed[c, pl.ds(0, PAD), :] = jnp.zeros((PAD, LANES), F32)
+    ss_own[...] = jnp.zeros(ss_own.shape, F32)
+    groups, reach = medium_taps.shape
+    share = LANES // (groups // n_ctx)
+    row = lax.broadcasted_iota(jnp.int32, (groups, LANES), 0)
+    lane = lax.broadcasted_iota(jnp.int32, (groups, LANES), 1)
+    chosen = jnp.where(row == ctx * (groups // n_ctx) + lane // share, 1.0, 0.0).astype(BF)
+    spread_taps = lax.dot_general(
+        medium_taps[...], chosen, (((0,), (0,)), ((), ())), preferred_element_type=F32
+    )
+    taps[1] = spread_taps.reshape(reach // 8, 8, LANES)
+    taps[0] = jnp.zeros((reach // 8, 8, LANES), F32)
+    count = short_taps.shape[0]
+    taps[0, 0, pl.ds(0, count), :] = short_taps[:, lanes(ctx)].astype(F32)
+    pl.semaphore_wait(barrier, guests)
+    own_load.wait()
 
     def hop_copy(source, q, j, upward):
         sems, device = (up_s, above) if upward else (down_s, below)
@@ -193,7 +225,7 @@
             keep_copy(source, j).start()
 
     def first(j):
-        source = stream.at[span(j), :]
+        source = land.at[chan, span(j), :]
 
         @pl.when(chan < last)
         def _():
@@ -205,31 +237,32 @@
 
         spread(source, chan, j)
 
-    def relay(j):
-        for distance in range(1, n_chan):
-            @pl.when(chan >= distance)
+    def relay(q, j, upward):
+        source = land.at[q, span(j), :]
+        hop_copy(source, q, j, upward).wait_recv()
+
+        @pl.when((chan < last) if upward else (chan > 0))
+        def _():
+            hop_copy(source, q, j, upward).start()
+
+        spread(source, q, j)
+
+    def relay_round(r):
+        for distance in range(last, 0, -1):
+            j = r - distance
+            present = (j >= 0) & (j < each_block)
+
+            @pl.when(present & (chan >= distance))
             def _():
-                q = chan - distance
-                source = land.at[q, span(j), :]
-                hop_copy(source, q, j, True).wait_recv()
-
-                @pl.when(chan < last)
-                def _():
-                    hop_copy(source, q, j, True).start()
-
-                spread(source, q, j)
-
-            @pl.when(chan + distance <= last)
+                relay(chan - distance, j, True)
+
+            @pl.when(present & (chan + distance <= last))
             def _():
-                q = chan + distance
-                source = land.at[q, span(j), :]
-                hop_copy(source, q, j, False).wait_recv()
-
-                @pl.when(chan > 0)
-                def _():
-                    hop_copy(source, q, j, False).start()
-
-                spread(source, q, j)
+                relay(chan + distance, j, False)
+
+        @pl.when(r < each_block)
+        def _():
+            first(r)
 
     def relay_settle(j):
         for q in range(n_chan):
@@ -250,11 +283,11 @@
     def first_arrive(t):
         @pl.when(t // each_block == ctx)
         def _():
-            pltpu.make_async_copy(stream.at[span(0), :], h.at[span(t), :], m_r.at[t]).wait()
+            pltpu.make_async_copy(land.at[0, span(0), :], h.at[span(t), :], m_r.at[t]).wait()
 
         @pl.when(t // each_block != ctx)
         def _():
-            remote(stream.at[span(0), :], h.at[span(t), :], m_s.at[0, 0], m_r.at[t], partner).wait_recv()
+            remote(land.at[0, span(0), :], h.at[span(t), :], m_s.at[0, 0], m_r.at[t], partner).wait_recv()
 
     def ss_copy(rel, t):
         return remote(ss_own.at[t], ss_recv.at[rel, t], ss_s.at[rel, t], ss_r.at[rel, t], relations[rel])
@@ -288,10 +321,7 @@
         return inner & ((s + 1 < STEPS) | home)
 
     def returns(s):
-        return inner & ((s + 1 < STEPS) | (ctx == near["chan"]))
-
-    def awaits(s):
-        return outer & ((s + 1 < STEPS) | corner)
+        return inner & (s + 1 < STEPS)
 
     def settle(s, t):
         for slot in range(2):
@@ -411,6 +441,20 @@
         def _():
             c_copy(s % 2, t).start()
 
+    def out_copy(t):
+        there = span(t % each_block)
+        return remote(
+            h.at[span(t), :], out.at[there, :], o_s.at[t], o_r.at[t % each_block],
+            {"ctx": t // each_block, "chan": ctx},
+        )
+
+    def keep_out(t):
+        there = span(t % each_block)
+        return pltpu.make_async_copy(h.at[span(t), :], out.at[there, :], o_s.at[t])
+
+    def stays(t):
+        return corner & (t // each_block == ctx)
+
     def update(s, t):
         @pl.when(takes(s))
         def _():
@@ -423,74 +467,54 @@
         def _():
             b_copy(t).start()
 
-    def out_copy(t):
-        there = span(t % each_block)
-        return remote(h.at[span(t), :], out.at[there, :], o_s.at[t], o_r.at[t % each_block], {"ctx": t // each_block})
-
-    def keep_out(t):
-        there = span(t % each_block)
-        return pltpu.make_async_copy(h.at[span(t), :], out.at[there, :], o_s.at[t])
-
-    def leave(s, t):
-        @pl.when((s + 1 == STEPS) & corner)
-        def _():
-            @pl.when(outer)
-            def _():
-                b_copy(t).wait_recv()
-
-            @pl.when(t // each_block != ctx)
-            def _():
-                out_copy(t).start()
-
-            @pl.when(t // each_block == ctx)
-            def _():
-                keep_out(t).start()
+        @pl.when((s + 1 == STEPS) & inner & home & jnp.logical_not(stays(t)))
+        def _():
+            out_copy(t).start()
+
+        @pl.when((s + 1 == STEPS) & inner & home & stays(t))
+        def _():
+            keep_out(t).start()
 
     stages = (
-        (ARRIVE, leave), (UPDATE, update), (MEET, meet), (DOT, dot), (MIX, mix), (CROSS, cross), (0, enter),
+        (UPDATE, update), (MEET, meet), (DOT, dot), (MIX, mix), (CROSS, cross), (0, enter),
     )
 
     def tick(u):
-        @pl.when(u < each_block)
-        def _():
-            relay(u)
-
         for lag, body in stages:
             @pl.when((u >= lag) & (u < items + lag))
             def _():
                 n = u - lag
                 body(n // CHUNKS, n % CHUNKS)
 
-    each(each_block, first)
-    in_load.start()
-    out_load.start()
-    for c in range(8):
-        mixed[c, pl.ds(0, PAD), :] = jnp.zeros((PAD, LANES), F32)
-    ss_own[...] = jnp.zeros(ss_own.shape, F32)
-    groups, reach = medium_taps.shape
-    share = LANES // (groups // n_ctx)
-    row = lax.broadcasted_iota(jnp.int32, (groups, LANES), 0)
-    lane = lax.broadcasted_iota(jnp.int32, (groups, LANES), 1)
-    chosen = jnp.where(row == ctx * (groups // n_ctx) + lane // share, 1.0, 0.0).astype(BF)
-    spread_taps = lax.dot_general(
-        medium_taps[...], chosen, (((0,), (0,)), ((), ())), preferred_element_type=F32
-    )
-    taps[1] = spread_taps.reshape(reach // 8, 8, LANES)
-    taps[0] = jnp.zeros((reach // 8, 8, LANES), F32)
-    count = short_taps.shape[0]
-    taps[0, 0, pl.ds(0, count), :] = short_taps[:, lanes(ctx)].astype(F32)
+        @pl.when((core == 0) & (u < each_block - 1))
+        def _():
+            relay_round(last + 1 + u)
+
+        @pl.when((core == 1) & (u < 2))
+        def _():
+            relay_round(u)
+
+        @pl.when((core == 1) & (u >= 2) & (u < 2 + each_block // 2 + 1))
+        def _():
+            for extra in range(2):
+                relay_round(2 * u - 2 + extra)
+
+    @pl.when(core == 0)
+    def _():
+        each(last + 1, relay_round)
+
     in_load.wait()
     out_load.wait()
-    each(items + ARRIVE, tick)
+    each(items + UPDATE, tick)
 
     def finish(t):
         settle(STEPS - 1, t)
 
-        @pl.when(corner & (t // each_block != ctx))
+        @pl.when(inner & home & jnp.logical_not(stays(t)))
         def _():
             out_copy(t).wait_send()
 
-        @pl.when(corner & (t // each_block == ctx))
+        @pl.when(inner & home & stays(t))
         def _():
             keep_out(t).wait()
 
@@ -499,7 +523,7 @@
     def received(j):
         relay_settle(j)
 
-        @pl.when(jnp.logical_not(corner))
+        @pl.when(jnp.logical_not(corner & inner))
         def _():
             out_copy(j).wait_recv()
 
@@ -547,14 +571,14 @@
         dma((CHUNKS,)), dma((CHUNKS,)),
         dma((2, CHUNKS)), dma((2, CHUNKS)),
         dma((CHUNKS,)), dma((CHUNKS,)),
-        dma((CHUNKS,)), dma((each_block,)), dma((2,)),
+        dma((CHUNKS,)), dma((each_block,)), dma((3,)),
     ]
     sizes = (tokens, rows, block, features * n_ctx)
     return pl.pallas_call(
         partial(wave_kernel, sizes),
         out_shape=jax.ShapeDtypeStruct(stream.shape, stream.dtype),
-        in_specs=[pl.BlockSpec(memory_space=pltpu.SMEM), vmem, anywhere, anywhere, vmem, vmem],
-        out_specs=vmem,
+        in_specs=[pl.BlockSpec(memory_space=pltpu.SMEM), anywhere, anywhere, anywhere, vmem, vmem],
+        out_specs=anywhere,
         scratch_shapes=scratch,
         compiler_params=pltpu.CompilerParams(
             collective_id=0, has_side_effects=True, vmem_limit_bytes=60 * 1024 * 1024

time: 200 us -> 195 us (0.975)
  Pallas kernels: 197 us -> 193 us
    pallas_call x1, Pallas kernels: 197 us -> 193 us  [wave(): pl.pallas_call(partial(wave_kernel, sizes), out_shape=jax.ShapeDtypeStruc...]
where the time goes in v3:
time: 195 us
  Pallas kernels  193 us (99%)
    pallas_call x1, Pallas kernels, wave(): pl.pallas_call(partial(wave_kernel, sizes), out_shape=jax.ShapeDtypeStruc...  193 us

profile of v3, /device:TPU:3, one launch (start us, length us, event | category | flops | bytes accessed | tf_op | source)
XLA Modules:
  0.0 194.9 jit_solution(4351735829900588474)
XLA Ops:
  0.0 193.1 %shard_map.64 = bf16[192,1024]{1,0:T(8,128)(2,1)} custom-call(s32[4]{0:T(128)} %plan.1, bf16[192,1024]{1,0:T(8,128)(2,1)} %stream_hbm.1, bf16[2,3,1024,512]{3,2,1,0:T(8,128)(2,1)} %bitcast.2, bf16[2,1024,512]{2,1,0:T(8,128)(2,1)} %w_out_hbm.1, bf16[7,512]{1,0:T(8,128)(2,1)} %short_taps.1, bf16[32,128]{1,0:T(8,128)(2,1)} %bitcast.3), custom_call_target="tpu_custom_call" | custom-call | tf_op jit(solution)/shard_map/pallas_call | solution.py:577
  193.1 1.8 copy.8

commit v4 on v3

--- a/solution.py
+++ b/solution.py
@@ -476,7 +476,7 @@
             keep_out(t).start()
 
     stages = (
-        (UPDATE, update), (MEET, meet), (DOT, dot), (MIX, mix), (CROSS, cross), (0, enter),
+        (CROSS, cross), (UPDATE, update), (MEET, meet), (DOT, dot), (MIX, mix), (0, enter),
     )
 
     def tick(u):

time: 195 us -> 206 us (1.056)
  Pallas kernels: 193 us -> 204 us
    pallas_call x1, Pallas kernels: 193 us -> 204 us  [wave(): pl.pallas_call(partial(wave_kernel, sizes), out_shape=jax.ShapeDtypeStruc...]
where the time goes in v4:
time: 206 us
  Pallas kernels  204 us (99%)
    pallas_call x1, Pallas kernels, wave(): pl.pallas_call(partial(wave_kernel, sizes), out_shape=jax.ShapeDtypeStruc...  204 us

profile of v4, /device:TPU:3, one launch (start us, length us, event | category | flops | bytes accessed | tf_op | source)
XLA Modules:
  0.0 206.1 jit_solution(1730449577600452739)
XLA Ops:
  0.0 204.4 %shard_map.64 = bf16[192,1024]{1,0:T(8,128)(2,1)} custom-call(s32[4]{0:T(128)} %plan.1, bf16[192,1024]{1,0:T(8,128)(2,1)} %stream_hbm.1, bf16[2,3,1024,512]{3,2,1,0:T(8,128)(2,1)} %bitcast.2, bf16[2,1024,512]{2,1,0:T(8,128)(2,1)} %w_out_hbm.1, bf16[7,512]{1,0:T(8,128)(2,1)} %short_taps.1, bf16[32,128]{1,0:T(8,128)(2,1)} %bitcast.3), custom_call_target="tpu_custom_call" | custom-call | tf_op jit(solution)/shard_map/pallas_call | solution.py:577
  204.4 1.8 copy.8
